TPU v7x, 32 devices: a whole 2x2x4 slice. The times are simulated.
32 devices in a mesh: gx: 4 (over z), gy: 8 (over y, x, core).
Axes of the slice: x: 2, y: 2, z: 4, core: 2. Of those that a mesh axis runs over, the one named last changes fastest.
Arguments:
- die_basis: float32 [64, 256, 512], P('gx', 'gy'), may hold values from -0.078125 to 0.078125
- die_coeff: float32 [5, 64, 256], P(None, 'gx', 'gy'), may hold values from 0.2 to 5
- pkg_basis: float32 [1024, 64, 512], P(('gx', 'gy')), may hold values from -0.09375 to 0.09375
- send_blocks: int32 [32, 4, 4], P(('gx', 'gy')), may hold values from 0 to 31
- columns: int32 [5, 1024, 4], P(None, ('gx', 'gy')), may hold values from 0 to 47
- counts: int32 [5, 1024], P(None, ('gx', 'gy')), may hold values from 1 to 4
- pkg_blocks: float32 [5, 1024, 64, 256], P(None, ('gx', 'gy')), may hold values from -48 to 48
Outputs:
- reduced: float32 [5, 512, 512], replicated
Inputs may be any that keep to these rules, and one draw needn't show every extreme that they name: `columns`: indices below 32 name the partition's own blocks, the others its ghost blocks in the order of the statement.
All inputs are finite; a program needn't handle non-finite values.
Results may differ from a plain program's by a relative error of at most 0.0001.
Values sent between devices are 32-bit elements; how exact they have to be, the bound alone decides.
No kernel may reach another device: no remote copies, remote signals or barrier semaphores. Data moves between devices by JAX's collectives and lax.ppermute only.
A program may use at most 256 MiB of HBM per device.

v0:
```python
import jax
import jax.numpy as jnp
from jax import lax
from jax.sharding import PartitionSpec as P

highest = lax.Precision.HIGHEST


def from_behind(value, axis, steps):
    count = lax.axis_size(axis)
    leading, last = (max(0, -steps), min(count, count - steps))
    return lax.ppermute(value, axis, [(source, source + steps) for source in range(leading, last)])


def passed_along(value, axis, steps):
    count = lax.axis_size(axis)
    pairs = [(source, (source + steps) % count) for source in range(count)]
    return lax.ppermute(value, axis, pairs)


def weighted_gram(weights, field):
    width = field.shape[-1]
    flat = field.reshape(-1, width)
    scaled = weights.reshape(-1, 1) * flat
    return lax.dot_general(
        flat,
        scaled,
        (((0,), (0,)), ((), ())),
        precision=highest,
        preferred_element_type=jnp.float32,
    )


def die_terms(basis, coeff, next_x_row, next_y_col):
    next_x = jnp.concatenate([basis[1:], next_x_row], axis=0)
    next_y = jnp.concatenate([basis[:, 1:], next_y_col], axis=1)
    diff_x = basis - next_x
    diff_y = basis - next_y
    return jnp.stack(
        [
            weighted_gram(coeff[0], basis),
            weighted_gram(coeff[1], diff_x),
            weighted_gram(coeff[2], diff_y),
            weighted_gram(coeff[3], basis),
            weighted_gram(coeff[4], diff_x) + weighted_gram(coeff[4], diff_y),
        ]
    )


def package_terms(owned, table, columns, counts, blocks):
    row_count = owned.shape[0]
    block = owned.shape[1]
    width = owned.shape[2]
    entries = columns.shape[-1]
    results = []
    for term_idx in range(columns.shape[0]):
        picked = table[columns[term_idx]]
        live = (jnp.arange(entries, dtype=jnp.int32)[None, :] < counts[term_idx][:, None]).astype(
            jnp.float32
        )
        matrices = (
            blocks[term_idx].reshape(row_count, block, entries, block) * live[:, None, :, None]
        )
        image = jnp.einsum("rinj,rnjk->rik", matrices, picked, precision=highest)
        results.append(
            lax.dot_general(
                owned.reshape(-1, width),
                image.reshape(-1, width),
                (((0,), (0,)), ((), ())),
                precision=highest,
                preferred_element_type=jnp.float32,
            )
        )
    return jnp.stack(results)


def body(die_basis, die_coeff, pkg_basis, send_blocks, columns, counts, pkg_blocks):
    next_x_row = from_behind(die_basis[:1], "gx", -1)
    next_y_col = from_behind(die_basis[:, :1], "gy", -1)
    lists = send_blocks[0]
    from_lower_x = passed_along(pkg_basis[lists[0]], "gx", 1)
    from_upper_x = passed_along(pkg_basis[lists[1]], "gx", -1)
    from_lower_y = passed_along(pkg_basis[lists[2]], "gy", 1)
    from_upper_y = passed_along(pkg_basis[lists[3]], "gy", -1)
    table = jnp.concatenate(
        [pkg_basis, from_lower_x, from_upper_x, from_lower_y, from_upper_y], axis=0
    )
    partial_terms = die_terms(die_basis, die_coeff, next_x_row, next_y_col)
    partial_terms = partial_terms + package_terms(pkg_basis, table, columns, counts, pkg_blocks)
    return lax.psum(partial_terms, ("gx", "gy"))


def solution(mesh):
    placed = (
        P("gx", "gy", None),
        P(None, "gx", "gy"),
        P(("gx", "gy"), None, None),
        P(("gx", "gy"), None, None),
        P(None, ("gx", "gy"), None),
        P(None, ("gx", "gy")),
        P(None, ("gx", "gy"), None, None),
    )
    return jax.shard_map(body, mesh=mesh, in_specs=placed, out_specs=P(), check_vma=False)
```

profile of v0, /device:TPU:0, one launch (start us, length us, event | category | flops | bytes accessed | tf_op | source)
XLA Modules:
  0.0 460.3 jit_solution(5091545625883094443)
XLA Ops:
  7.4 3.6 gather_fusion
  11.0 3.1 collective-permute-start.2
  14.0 3.6 gather_fusion.1
  17.6 2.0 collective-permute-start.3
  19.6 3.6 gather_fusion.2
  23.2 3.6 gather_fusion.3
  26.8 2.6 collective-permute-start.5
  30.8 4.9 %constant_dynamic-update-slice_fusion.4 = f32[48,64,512]{2,1,0:T(8,128)} fusion(f32[32,64,512]{2,1,0:T(8,128)} %param.9), kind=kLoop, calls=%fused_computation.81 | loop fusion | bytes 8388608
  36.1 7.9 %fusion.120 = (f32[1,32,64,256]{3,2,1,0:T(8,128)S(1)}, f32[1,32,64,256]{3,2,1,0:T(8,128)}, f32[1,32,64,256]{3,2,1,0:T(8,128)}, f32[1,32,64,256]{3,2,1,0:T(8,128)}, f32[1,32,64,256]{3,2,1,0:T(8,128)}) fusion(f32[5,32,64,256]{3,2,1,0:T(8,128)} %param.13), kind=kLoop, calls=%fused_computation.128 | loop fusion | bytes 20971520 | tf_op jit(solution)/shard_map/slice | solution.py:62
  44.0 5.1 %reshape_squeeze.22 = f32[32,64,4,64]{3,2,1,0:T(4,128)} reshape(f32[1,32,64,256]{3,2,1,0:T(8,128)} %get-tuple-element.7) | data formatting | bytes 4194304 | tf_op jit(solution)/shard_map/reshape;squeeze | solution.py:62
  49.3 5.1 %reshape_squeeze.10 = f32[32,64,4,64]{3,2,1,0:T(4,128)} reshape(f32[1,32,64,256]{3,2,1,0:T(8,128)} %get-tuple-element.8) | data formatting | bytes 4194304 | tf_op jit(solution)/shard_map/reshape;squeeze | solution.py:62
  54.3 5.1 %reshape_squeeze.23 = f32[32,64,4,64]{3,2,1,0:T(4,128)} reshape(f32[1,32,64,256]{3,2,1,0:T(8,128)} %get-tuple-element.6) | data formatting | bytes 4194304 | tf_op jit(solution)/shard_map/reshape;squeeze | solution.py:62
  59.8 5.1 %reshape_squeeze.24 = f32[32,64,4,64]{3,2,1,0:T(4,128)} reshape(f32[1,32,64,256]{3,2,1,0:T(8,128)} %get-tuple-element.9) | data formatting | bytes 4194304 | tf_op jit(solution)/shard_map/reshape;squeeze | solution.py:62
  64.9 3.5 reshape_squeeze.25
  68.5 2.0 fusion.35
  70.6 2.9 broadcast_multiply_fusion.3
  73.5 2.9 broadcast_multiply_fusion.4
  76.6 2.9 broadcast_multiply_fusion.2
  79.5 2.9 broadcast_multiply_fusion.1
  82.5 3.0 broadcast_multiply_fusion
  87.2 2.2 fusion.59
  89.4 3.0 collective-permute-done
  92.4 2.1 fusion.41
  94.5 2.2 fusion.47
  96.8 2.0 fusion.53
  98.8 2.2 fusion.98
  101.0 2.3 copy-done.10
  105.2 1.9 constant_dynamic-update-slice_fusion.2
  107.1 1.9 constant_dynamic-update-slice_fusion.1
  109.0 1.9 constant_dynamic-update-slice_fusion
  110.8 12.9 %gather_fusion.5 = f32[128,64,512]{2,1,0:T(8,128)} fusion(f32[48,64,512]{2,1,0:T(8,128)} %constant_dynamic-update-slice_fusion, s32[1024]{0:T(1024)S(1)} %get-tuple-element.32), kind=kCustom, calls=%fused_computation.5 | custom fusion | bytes 33554944 | tf_op jit(solution)/shard_map/gather | solution.py:57
  123.7 12.7 %gather_fusion.4 = f32[128,64,512]{2,1,0:T(8,128)} fusion(f32[48,64,512]{2,1,0:T(8,128)} %constant_dynamic-update-slice_fusion, s32[1024]{0:T(1024)S(1)} %pad_clamp_fusion.4), kind=kCustom, calls=%fused_computation.4 | custom fusion | bytes 33554944 | tf_op jit(solution)/shard_map/gather | solution.py:57
  136.4 13.9 %fusion.18 = f32[32,64,512,1]{2,1,3,0:T(8,128)S(1)} fusion(f32[32,4,64,512]{3,2,1,0:T(8,128)} %bitcast.211, f32[32,64,4,64]{3,2,1,0:T(4,128)} %broadcast_multiply_fusion.4), kind=kOutput, calls=%fused_computation.27 | convolution fusion | flops 3221225472 | bytes 23068672 | tf_op jit(solution)/shard_map/rinj,rnjk->rik/dot_general | solution.py:64
  150.4 8.0 %fusion.65 = f32[5,512,512]{1,2,0:T(8,128)} fusion(f32[32,64,512]{2,1,0:T(8,128)S(1)} %copy-done.9, f32[32,64,512,1]{2,1,3,0:T(8,128)S(1)} %fusion.18), kind=kOutput, calls=%fused_computation.57 | convolution fusion | flops 6442450944 | bytes 9437184 | tf_op jit(solution)/shard_map/dot_general | solution.py:66
  158.3 12.7 %gather_fusion.6 = f32[128,64,512]{2,1,0:T(8,128)} fusion(f32[48,64,512]{2,1,0:T(8,128)} %constant_dynamic-update-slice_fusion, s32[1024]{0:T(1024)S(1)} %get-tuple-element.31), kind=kCustom, calls=%fused_computation.6 | custom fusion | bytes 33554944 | tf_op jit(solution)/shard_map/gather | solution.py:57
  171.0 12.7 %gather_fusion.7 = f32[128,64,512]{2,1,0:T(8,128)} fusion(f32[48,64,512]{2,1,0:T(8,128)} %constant_dynamic-update-slice_fusion, s32[1024]{0:T(1024)S(1)} %get-tuple-element.30), kind=kCustom, calls=%fused_computation.7 | custom fusion | bytes 33554944 | tf_op jit(solution)/shard_map/gather | solution.py:57
  183.7 12.9 %gather_fusion.8 = f32[128,64,512]{2,1,0:T(8,128)} fusion(f32[48,64,512]{2,1,0:T(8,128)} %constant_dynamic-update-slice_fusion, s32[1024]{0:T(1024)S(1)} %get-tuple-element.29), kind=kCustom, calls=%fused_computation.8 | custom fusion | bytes 33554944 | tf_op jit(solution)/shard_map/gather | solution.py:57
  196.5 16.1 %fusion.16 = f32[32,64,512,1]{2,1,3,0:T(8,128)} fusion(f32[32,4,64,512]{3,2,1,0:T(8,128)} %bitcast.206, f32[32,64,4,64]{3,2,1,0:T(4,128)} %broadcast_multiply_fusion.3), kind=kOutput, calls=%fused_computation.25 | convolution fusion | flops 3221225472 | bytes 23068672 | tf_op jit(solution)/shard_map/rinj,rnjk->rik/dot_general | solution.py:64
  212.6 10.4 %fusion.71 = f32[5,512,512]{1,2,0:T(8,128)} fusion(f32[5,512,512]{1,2,0:T(8,128)} %fusion.65, f32[32,64,512]{2,1,0:T(8,128)} %param.9, f32[32,64,512,1]{2,1,3,0:T(8,128)} %fusion.16), kind=kOutput, calls=%fused_computation.59 | convolution fusion | flops 6442450944 | bytes 9437184 | tf_op jit(solution)/shard_map/dot_general | solution.py:66
  223.0 12.0 %fusion.14 = f32[32,64,512,1]{2,1,3,0:T(8,128)} fusion(f32[32,4,64,512]{3,2,1,0:T(8,128)S(1)} %bitcast.210, f32[32,64,4,64]{3,2,1,0:T(4,128)S(1)} %copy-done.6), kind=kOutput, calls=%fused_computation.23 | convolution fusion | flops 3221225472 | bytes 23068672 | tf_op jit(solution)/shard_map/rinj,rnjk->rik/dot_general | solution.py:64
  235.1 10.4 %fusion.77 = f32[5,512,512]{1,2,0:T(8,128)} fusion(f32[5,512,512]{1,2,0:T(8,128)} %fusion.71, f32[32,64,512]{2,1,0:T(8,128)} %param.9, f32[32,64,512,1]{2,1,3,0:T(8,128)} %fusion.14), kind=kOutput, calls=%fused_computation.61 | convolution fusion | flops 6442450944 | bytes 9437184 | tf_op jit(solution)/shard_map/dot_general | solution.py:66
  245.5 14.7 %fusion.12 = f32[32,64,512,1]{2,1,3,0:T(8,128)} fusion(f32[32,4,64,512]{3,2,1,0:T(8,128)} %bitcast.207, f32[32,64,4,64]{3,2,1,0:T(4,128)S(1)} %copy-done.8), kind=kOutput, calls=%fused_computation.21 | convolution fusion | flops 3221225472 | bytes 23068672 | tf_op jit(solution)/shard_map/rinj,rnjk->rik/dot_general | solution.py:64
  260.2 10.6 %fusion.83 = f32[5,512,512]{1,2,0:T(8,128)} fusion(f32[5,512,512]{1,2,0:T(8,128)} %fusion.77, f32[32,64,512]{2,1,0:T(8,128)} %param.9, f32[32,64,512,1]{2,1,3,0:T(8,128)} %fusion.12), kind=kOutput, calls=%fused_computation.63 | convolution fusion | flops 6442450944 | bytes 9437184 | tf_op jit(solution)/shard_map/dot_general | solution.py:66
  270.8 11.8 %fusion.10 = f32[32,64,512,1]{2,1,3,0:T(8,128)} fusion(f32[32,4,64,512]{3,2,1,0:T(8,128)S(1)} %bitcast.205, f32[32,64,4,64]{3,2,1,0:T(4,128)S(1)} %copy-done.7), kind=kOutput, calls=%fused_computation.19 | convolution fusion | flops 3221225472 | bytes 23068672 | tf_op jit(solution)/shard_map/rinj,rnjk->rik/dot_general | solution.py:64
  282.6 10.2 %fusion.89 = f32[5,512,512]{1,2,0:T(8,128)} fusion(f32[5,512,512]{1,2,0:T(8,128)} %fusion.83, f32[32,64,512]{2,1,0:T(8,128)} %param.9, f32[32,64,512,1]{2,1,3,0:T(8,128)} %fusion.10), kind=kOutput, calls=%fused_computation.65 | convolution fusion | flops 6442450944 | bytes 9437184 | tf_op jit(solution)/shard_map/dot_general | solution.py:66
  292.9 7.9 %add.108 = f32[5,512,512]{1,2,0:T(8,128)} add(f32[5,512,512]{1,2,0:T(8,128)} %copy-done.10, f32[5,512,512]{1,2,0:T(8,128)} %fusion.89) | non-fusion elementwise | flops 1310720 | bytes 15728640 | tf_op jit(solution)/shard_map/add | solution.py:89
  300.8 146.3 %all-reduce.2.cloned.1.call-done = f32[5,512,512]{1,2,0:T(8,128)} async-done(((f32[5,512,512]{1,2,0:T(8,128)}), f32[5,512,512]{1,2,0:T(8,128)}) %all-reduce.2.cloned.1.call-update) | async-done | bytes 5242896 | tf_op jit(solution)/shard_map/psum | solution.py:90
  447.1 5.9 %copy.27 = f32[5,512,512]{2,1,0:T(8,128)} copy(f32[5,512,512]{1,2,0:T(8,128)} %all-reduce.2.cloned.1.call-done) | data formatting | bytes 10485760 | tf_op jit(solution)/shard_map/psum | solution.py:90
  (84 shorter events, 7.1 us)
Async XLA Ops:
  6.5 22.9 %copy-start = (f32[16,32,512]{2,1,0:T(8,128)S(1)}, f32[16,32,512]{2,1,0:T(8,128)}, u32[]{:S(2)}) copy-start(f32[16,32,512]{2,1,0:T(8,128)} %param.7) | copy-start | bytes 3145732
  6.5 440.6 %all-reduce.2.cloned.1.call-start = ((), (), s32[]{:S(2)}) async-start(), calls=%async_computation | async-start | bytes 10485760 | tf_op jit(solution)/shard_map/psum | solution.py:90
  11.0 92.4 %collective-permute-start.2 = (f32[4,64,512]{2,1,0:T(8,128)}, f32[4,64,512]{2,1,0:T(8,128)}, u32[]{:S(2)}, u32[]{:S(2)}) collective-permute-start(f32[4,64,512]{2,1,0:T(8,128)} %gather_fusion), channel_id=1, source_target_pairs={{0,8},{8,16},{16,24},{24,0},{1,9},{9,17},{17,25},{25,1},{2,10},{10... | collective-permute-start | bytes 1572872 | tf_op jit(solution)/shard_map/ppermute | solution.py:18
  17.6 87.6 %collective-permute-start.3 = (f32[4,64,512]{2,1,0:T(8,128)}, f32[4,64,512]{2,1,0:T(8,128)}, u32[]{:S(2)}, u32[]{:S(2)}) collective-permute-start(f32[4,64,512]{2,1,0:T(8,128)} %gather_fusion.1), channel_id=1, source_target_pairs={{0,24},{8,0},{16,8},{24,16},{1,25},{9,1},{17,9},{25,17},{2,26},{10... | collective-permute-start | bytes 1572872 | tf_op jit(solution)/shard_map/ppermute | solution.py:18
  23.2 83.9 %collective-permute-start.4 = (f32[4,64,512]{2,1,0:T(8,128)}, f32[4,64,512]{2,1,0:T(8,128)}, u32[]{:S(2)}, u32[]{:S(2)}) collective-permute-start(f32[4,64,512]{2,1,0:T(8,128)} %gather_fusion.2), channel_id=1, source_target_pairs={{0,1},{1,2},{2,3},{3,4},{4,5},{5,6},{6,7},{7,0},{8,9},{9,10},{10,1... | collective-permute-start | bytes 1572872 | tf_op jit(solution)/shard_map/ppermute | solution.py:18
  26.8 82.2 %collective-permute-start.5 = (f32[4,64,512]{2,1,0:T(8,128)}, f32[4,64,512]{2,1,0:T(8,128)}, u32[]{:S(2)}, u32[]{:S(2)}) collective-permute-start(f32[4,64,512]{2,1,0:T(8,128)} %gather_fusion.3), channel_id=1, source_target_pairs={{0,7},{1,0},{2,1},{3,2},{4,3},{5,4},{6,5},{7,6},{8,15},{9,8},{10,9... | collective-permute-start | bytes 1572872 | tf_op jit(solution)/shard_map/ppermute | solution.py:18
  29.5 6.2 %copy-start.12 = (s32[5,32,4]{1,2,0:T(4,128)S(1)}, s32[5,32,4]{1,2,0:T(4,128)}, u32[]{:S(2)}) copy-start(s32[5,32,4]{1,2,0:T(4,128)} %param.11) | copy-start | bytes 7684
  29.5 6.6 %copy-start.13 = (s32[5,32]{1,0:T(8,128)S(1)}, s32[5,32]{1,0:T(8,128)}, u32[]{:S(2)}) copy-start(s32[5,32]{1,0:T(8,128)} %param.12) | copy-start | bytes 1924
  29.5 56.2 %collective-permute-start.1 = (f32[16,1,512]{2,1,0:T(1,128)S(1)}, f32[16,1,512]{2,1,0:T(1,128)S(1)}, u32[]{:S(2)}, u32[]{:S(2)}) collective-permute-start(f32[16,1,512]{2,1,0:T(1,128)S(1)} %slice.94), channel_id=1, source_target_pairs={{1,0},{2,1},{3,2},{4,3},{5,4},{6,5},{7,6},{9,8},{10,9},{11,10},{12... | collective-permute-start | bytes 98312 | tf_op jit(solution)/shard_map/ppermute | solution.py:12
  64.9 3.6 copy-start.11
  68.4 2.2 copy-start.4
  70.6 2.9 copy-start.5
  73.5 3.0 copy-start.1
  76.6 3.0 copy-start.2
  79.5 2.9 copy-start.3
  85.7 6.7 %collective-permute-start = (f32[1,32,512]{2,1,0:T(8,128)S(1)}, f32[1,32,512]{2,1,0:T(8,128)S(1)}, u32[]{:S(2)}, u32[]{:S(2)}) collective-permute-start(f32[1,32,512]{2,1,0:T(8,128)S(1)} %slice.91), channel_id=1, source_target_pairs={{8,0},{16,8},{24,16},{9,1},{17,9},{25,17},{10,2},{18,10},{26,18},{... | collective-permute-start | bytes 196616 | tf_op jit(solution)/shard_map/ppermute | solution.py:12
  101.0 2.4 copy-start.10
  136.4 14.0 %copy-start.9 = (f32[32,64,512]{2,1,0:T(8,128)S(1)}, f32[32,64,512]{2,1,0:T(8,128)}, u32[]{:S(2)}) copy-start(f32[32,64,512]{2,1,0:T(8,128)} %param.9) | copy-start | bytes 12582916
  196.5 26.5 %slice-start.4 = ((s8[16777216]{0:T(1024)(128)(4,1)}), s8[4194304]{0:T(1024)(128)(4,1)S(1)}, s32[]{:S(2)}) async-start(s8[16777216]{0:T(1024)(128)(4,1)} %bitcast.208), calls=%async_computation.5 | async-start | bytes 8388608
  196.5 26.5 %slice-start.5 = ((s8[16777216]{0:T(1024)(128)(4,1)}), s8[4194304]{0:T(1024)(128)(4,1)S(1)}, s32[]{:S(2)}) async-start(s8[16777216]{0:T(1024)(128)(4,1)} %bitcast.208), calls=%async_computation.6 | async-start | bytes 8388608
  196.5 26.5 %slice-start.6 = ((s8[16777216]{0:T(1024)(128)(4,1)}), s8[4194304]{0:T(1024)(128)(4,1)S(1)}, s32[]{:S(2)}) async-start(s8[16777216]{0:T(1024)(128)(4,1)} %bitcast.208), calls=%async_computation.7 | async-start | bytes 8388608
  212.6 10.4 %slice-start.7 = ((s8[16777216]{0:T(1024)(128)(4,1)}), s8[4194304]{0:T(1024)(128)(4,1)S(1)}, s32[]{:S(2)}) async-start(s8[16777216]{0:T(1024)(128)(4,1)} %bitcast.208), calls=%async_computation.8 | async-start | bytes 8388608
  212.6 10.4 %copy-start.6 = (f32[32,64,4,64]{3,2,1,0:T(4,128)S(1)}, f32[32,64,4,64]{3,2,1,0:T(4,128)}, u32[]{:S(2)}) copy-start(f32[32,64,4,64]{3,2,1,0:T(4,128)} %broadcast_multiply_fusion.2) | copy-start | bytes 6291460
  235.1 10.4 %copy-start.8 = (f32[32,64,4,64]{3,2,1,0:T(4,128)S(1)}, f32[32,64,4,64]{3,2,1,0:T(4,128)}, u32[]{:S(2)}) copy-start(f32[32,64,4,64]{3,2,1,0:T(4,128)} %broadcast_multiply_fusion.1) | copy-start | bytes 6291460
  245.5 25.3 %slice-start = ((s8[16777216]{0:T(1024)(128)(4,1)}), s8[4194304]{0:T(1024)(128)(4,1)S(1)}, s32[]{:S(2)}) async-start(s8[16777216]{0:T(1024)(128)(4,1)} %bitcast.203), calls=%async_computation.1 | async-start | bytes 8388608
  245.5 25.3 %slice-start.1 = ((s8[16777216]{0:T(1024)(128)(4,1)}), s8[4194304]{0:T(1024)(128)(4,1)S(1)}, s32[]{:S(2)}) async-start(s8[16777216]{0:T(1024)(128)(4,1)} %bitcast.203), calls=%async_computation.2 | async-start | bytes 8388608
  245.5 25.3 %slice-start.2 = ((s8[16777216]{0:T(1024)(128)(4,1)}), s8[4194304]{0:T(1024)(128)(4,1)S(1)}, s32[]{:S(2)}) async-start(s8[16777216]{0:T(1024)(128)(4,1)} %bitcast.203), calls=%async_computation.3 | async-start | bytes 8388608
  260.2 10.6 %slice-start.3 = ((s8[16777216]{0:T(1024)(128)(4,1)}), s8[4194304]{0:T(1024)(128)(4,1)S(1)}, s32[]{:S(2)}) async-start(s8[16777216]{0:T(1024)(128)(4,1)} %bitcast.203), calls=%async_computation.4 | async-start | bytes 8388608
  260.2 10.6 %copy-start.7 = (f32[32,64,4,64]{3,2,1,0:T(4,128)S(1)}, f32[32,64,4,64]{3,2,1,0:T(4,128)}, u32[]{:S(2)}) copy-start(f32[32,64,4,64]{3,2,1,0:T(4,128)} %broadcast_multiply_fusion) | copy-start | bytes 6291460
Sparse Core Ops, SparseCore 0:
  301.0 146.1 all-reduce.1
where the time goes:
time: 468 us; the launch traced here: 460 us
  waiting for transfers between devices  149 us (32%)
  local copies, waits for them, and re-layouts  132 us (28%)
  matrix products  131 us (28%)
  other arithmetic  23.7 us (5%)
  between operations  14.2 us (3%)
  starting transfers between devices  10.5 us (2%)
    psum x1, waiting for transfers between devices, body(): return lax.psum(partial_terms, ('gx', 'gy'))  146 us
    dot_general x5, matrix products, package_terms(): image = jnp.einsum('rinj,rnjk->rik', matrices, picked, precision=highest)  68.6 us
    gather x5, local copies, waits for them, and re-layouts, package_terms(): picked = table[columns[term_idx]]  63.7 us
    dot_general x5, matrix products, package_terms(): lax.dot_general(owned.reshape(-1, width), image.reshape(-1, width), (((0,...  49.6 us
    another operation x5, local copies, waits for them, and re-layouts, package_terms(): blocks[term_idx].reshape(row_count, block, entries, block)  23.8 us
    mul x5, other arithmetic, package_terms(): blocks[term_idx].reshape(row_count, block, entries, block)  14.7 us
    unnamed x48, local copies, waits for them, and re-layouts  13 us
    dot_general x6, matrix products, weighted_gram(): lax.dot_general(flat, scaled, (((0,), (0,)), ((), ())), precision=highest...  12.7 us
  transfers between devices with their start and end apart: 7, of which 2 were waited for; matrix products, arithmetic and copies ran while one was open for 18% of the time, Pallas kernels for 0%

commit v1 on v0

--- a/solution.py
+++ b/solution.py
@@ -87,7 +87,7 @@
     )
     partial_terms = die_terms(die_basis, die_coeff, next_x_row, next_y_col)
     partial_terms = partial_terms + package_terms(pkg_basis, table, columns, counts, pkg_blocks)
-    return lax.psum(partial_terms, ("gx", "gy"))
+    return jnp.sum(lax.all_gather(partial_terms, ("gx", "gy")), axis=0)
 
 
 def solution(mesh):

time: 468 us -> 1210 us (2.59)
  waiting for transfers between devices: 149 us -> 840 us
  other arithmetic: 23.7 us -> 62.8 us
    all_gather x0 -> x1, waiting for transfers between devices: none -> 840 us  [body(): return jnp.sum(lax.all_gather(partial_terms, ('gx', 'gy')), axis=0)]
    psum x1 -> x0, waiting for transfers between devices: 146 us -> none  [body(): return lax.psum(partial_terms, ('gx', 'gy'))]
    reduce_sum x0 -> x1, other arithmetic: none -> 53.2 us  [body(): return jnp.sum(lax.all_gather(partial_terms, ('gx', 'gy')), axis=0)]
    mul x5 -> x0, other arithmetic: 14.7 us -> none  [package_terms(): blocks[term_idx].reshape(row_count, block, entries, block)]
  transfers between devices with their start and end apart: 7 -> 7, of which waited for: 2 -> 1; matrix products, arithmetic and copies ran while one was open for 18% -> 7% of each run, Pallas kernels for 0% -> 0%
where the time goes in v1:
time: 1210 us; the launch traced here: 1200 us
  waiting for transfers between devices  840 us (69%)
  matrix products  138 us (11%)
  local copies, waits for them, and re-layouts  132 us (11%)
  other arithmetic  62.8 us (5%)
  between operations  13.9 us (1%)
  starting transfers between devices  12.1 us (1%)
    all_gather x1, waiting for transfers between devices, body(): return jnp.sum(lax.all_gather(partial_terms, ('gx', 'gy')), axis=0)  840 us
    dot_general x5, matrix products, package_terms(): image = jnp.einsum('rinj,rnjk->rik', matrices, picked, precision=highest)  70.9 us
    gather x5, local copies, waits for them, and re-layouts, package_terms(): picked = table[columns[term_idx]]  63.6 us
    reduce_sum x1, other arithmetic, body(): return jnp.sum(lax.all_gather(partial_terms, ('gx', 'gy')), axis=0)  53.2 us
    dot_general x5, matrix products, package_terms(): lax.dot_general(owned.reshape(-1, width), image.reshape(-1, width), (((0,...  50.1 us
    another operation x5, local copies, waits for them, and re-layouts, package_terms(): blocks[term_idx].reshape(row_count, block, entries, block)  25.3 us
  transfers between devices with their start and end apart: 7, of which 1 were waited for; matrix products, arithmetic and copies ran while one was open for 7% of the time, Pallas kernels for 0%

profile of v1, /device:TPU:0, one launch (start us, length us, event | category | flops | bytes accessed | tf_op | source)
XLA Modules:
  0.0 1199.4 jit_solution(7505515507032009520)
XLA Ops:
  6.5 1.0 slice.94
  7.5 1.3 collective-permute-start.1
  8.8 0.8 slice.91
  9.7 1.3 collective-permute-start
  10.9 0.8 fusion.115
  11.8 3.6 gather_fusion.3
  15.4 4.7 collective-permute-start.5
  20.1 3.7 gather_fusion.1
  23.7 4.4 collective-permute-start.3
  28.1 3.5 gather_fusion
  31.7 4.9 constant_dynamic-update-slice_fusion.4
  37.7 2.9 fusion.35
  40.6 8.2 fusion.120
  48.9 0.7 fusion.109
  49.9 3.6 gather_fusion.2
  53.5 5.1 reshape_squeeze.25
  58.6 5.1 reshape_squeeze.23
  63.7 5.1 reshape_squeeze.22
  68.7 5.1 reshape_squeeze.10
  73.8 5.1 reshape_squeeze.24
  79.3 2.2 fusion.59
  81.5 3.1 fusion.41
  84.6 3.1 fusion.47
  87.7 2.9 fusion.53
  90.6 3.1 fusion.98
  93.7 1.9 constant_dynamic-update-slice_fusion.3
  95.6 1.9 constant_dynamic-update-slice_fusion.2
  97.5 0.8 constant_dynamic-update-slice_fusion.1
  98.3 1.9 constant_dynamic-update-slice_fusion
  100.2 12.9 %gather_fusion.8 = f32[128,64,512]{2,1,0:T(8,128)} fusion(f32[48,64,512]{2,1,0:T(8,128)} %constant_dynamic-update-slice_fusion, s32[1024]{0:T(1024)S(1)} %get-tuple-element.29), kind=kCustom, calls=%fused_computation.8 | custom fusion | bytes 33554944 | tf_op jit(solution)/shard_map/gather | solution.py:57
  113.0 12.7 %gather_fusion.7 = f32[128,64,512]{2,1,0:T(8,128)} fusion(f32[48,64,512]{2,1,0:T(8,128)} %constant_dynamic-update-slice_fusion, s32[1024]{0:T(1024)S(1)} %get-tuple-element.30), kind=kCustom, calls=%fused_computation.7 | custom fusion | bytes 33554944 | tf_op jit(solution)/shard_map/gather | solution.py:57
  125.7 12.7 %gather_fusion.6 = f32[128,64,512]{2,1,0:T(8,128)} fusion(f32[48,64,512]{2,1,0:T(8,128)} %constant_dynamic-update-slice_fusion, s32[1024]{0:T(1024)S(1)} %get-tuple-element.31), kind=kCustom, calls=%fused_computation.6 | custom fusion | bytes 33554944 | tf_op jit(solution)/shard_map/gather | solution.py:57
  138.4 12.7 %gather_fusion.5 = f32[128,64,512]{2,1,0:T(8,128)} fusion(f32[48,64,512]{2,1,0:T(8,128)} %constant_dynamic-update-slice_fusion, s32[1024]{0:T(1024)S(1)} %get-tuple-element.32), kind=kCustom, calls=%fused_computation.5 | custom fusion | bytes 33554944 | tf_op jit(solution)/shard_map/gather | solution.py:57
  151.1 12.8 %gather_fusion.4 = f32[128,64,512]{2,1,0:T(8,128)} fusion(f32[48,64,512]{2,1,0:T(8,128)} %constant_dynamic-update-slice_fusion, s32[1024]{0:T(1024)S(1)} %pad_clamp_fusion.4), kind=kCustom, calls=%fused_computation.4 | custom fusion | bytes 33554944 | tf_op jit(solution)/shard_map/gather | solution.py:57
  163.8 14.5 %fusion.14 = f32[32,64,512,1]{2,1,3,0:T(8,128)S(1)} fusion(f32[32,4,64,512]{3,2,1,0:T(8,128)} %bitcast.213, f32[32,64,4,64]{3,2,1,0:T(4,128)} %reshape_squeeze.10, f32[32,4]{1,0:T(8,128)S(1)} %get-tuple-element.33), kind=kOutput, calls=%fused_computation.28 | convolution fusion | flops 3221749760 | bytes 23069184 | tf_op jit(solution)/shard_map/rinj,rnjk->rik/dot_general | solution.py:64
  178.4 8.0 fusion.65
  186.4 15.3 %fusion.13 = f32[32,64,512,1]{2,1,3,0:T(8,128)} fusion(f32[32,4,64,512]{3,2,1,0:T(8,128)} %bitcast.212, f32[32,64,4,64]{3,2,1,0:T(4,128)S(1)} %copy-done.4, f32[32,4]{1,0:T(8,128)S(1)} %get-tuple-element.34), kind=kOutput, calls=%fused_computation.26 | convolution fusion | flops 3221749760 | bytes 23069184 | tf_op jit(solution)/shard_map/rinj,rnjk->rik/dot_general | solution.py:64
  201.7 10.8 fusion.71
  212.6 13.3 %fusion.12 = f32[32,64,512,1]{2,1,3,0:T(8,128)} fusion(f32[32,4,64,512]{3,2,1,0:T(8,128)S(1)} %bitcast.211, f32[32,64,4,64]{3,2,1,0:T(4,128)S(1)} %copy-done.3, f32[32,4]{1,0:T(8,128)} %get-tuple-element.35), kind=kOutput, calls=%fused_computation.24 | convolution fusion | flops 3221749760 | bytes 23069184 | tf_op jit(solution)/shard_map/rinj,rnjk->rik/dot_general | solution.py:64
  225.8 10.5 fusion.77
  236.4 15.3 %fusion.11 = f32[32,64,512,1]{2,1,3,0:T(8,128)} fusion(f32[32,4,64,512]{3,2,1,0:T(8,128)} %bitcast.208, f32[32,64,4,64]{3,2,1,0:T(4,128)S(1)} %copy-done.2, f32[32,4]{1,0:T(8,128)S(1)} %get-tuple-element.36), kind=kOutput, calls=%fused_computation.22 | convolution fusion | flops 3221749760 | bytes 23069184 | tf_op jit(solution)/shard_map/rinj,rnjk->rik/dot_general | solution.py:64
  251.7 10.4 fusion.83
  262.1 12.6 %fusion.10 = f32[32,64,512,1]{2,1,3,0:T(8,128)} fusion(f32[32,4,64,512]{3,2,1,0:T(8,128)S(1)} %bitcast.207, f32[32,64,4,64]{3,2,1,0:T(4,128)S(1)} %copy-done.1, f32[32,4]{1,0:T(8,128)S(1)} %fusion.111), kind=kOutput, calls=%fused_computation.20 | convolution fusion | flops 3221749760 | bytes 23069184 | tf_op jit(solution)/shard_map/rinj,rnjk->rik/dot_general | solution.py:64
  274.6 10.4 fusion.89
  285.0 7.9 add.113
  293.0 5.9 copy.40
  298.9 840.3 %all-gather.2.cloned.1.call-done = f32[32,5,512,512]{3,2,1,0:T(8,128)} async-done(((f32[1,5,512,512]{3,2,1,0:T(8,128)}), f32[32,5,512,512]{3,2,1,0:T(8,128)}) %all-gather.2.cloned.1.call-update) | async-done | bytes 167772176 | tf_op jit(solution)/shard_map/all_gather | solution.py:90
  1139.2 53.2 %reduce_sum.9 = f32[5,512,512]{2,1,0:T(8,128)} reduce(f32[32,5,512,512]{3,2,1,0:T(8,128)} %all-gather.2.cloned.1.call-done, f32[]{:T(128)} %constant.2.clone.1), dimensions={0}, to_apply=%region_0.0 | reduce | flops 40632320 | bytes 173015040 | tf_op jit(solution)/shard_map/reduce_sum | solution.py:90
  (70 shorter events, 2.0 us)
Async XLA Ops:
  6.5 1132.7 %all-gather.2.cloned.1.call-start = ((), (), s32[]{:S(2)}) async-start(), calls=%async_computation | async-start | bytes 173015040 | tf_op jit(solution)/shard_map/all_gather | solution.py:90
  7.5 71.3 %collective-permute-start.1 = (f32[16,1,512]{2,1,0:T(1,128)S(1)}, f32[16,1,512]{2,1,0:T(1,128)S(1)}, u32[]{:S(2)}, u32[]{:S(2)}) collective-permute-start(f32[16,1,512]{2,1,0:T(1,128)S(1)} %slice.94), channel_id=1, source_target_pairs={{1,0},{2,1},{3,2},{4,3},{5,4},{6,5},{7,6},{9,8},{10,9},{11,10},{12... | collective-permute-start | bytes 98312 | tf_op jit(solution)/shard_map/ppermute | solution.py:12
  9.7 71.8 %collective-permute-start = (f32[1,32,512]{2,1,0:T(8,128)S(1)}, f32[1,32,512]{2,1,0:T(8,128)S(1)}, u32[]{:S(2)}, u32[]{:S(2)}) collective-permute-start(f32[1,32,512]{2,1,0:T(8,128)S(1)} %slice.91), channel_id=1, source_target_pairs={{8,0},{16,8},{24,16},{9,1},{17,9},{25,17},{10,2},{18,10},{26,18},{... | collective-permute-start | bytes 196616 | tf_op jit(solution)/shard_map/ppermute | solution.py:12
  15.4 82.9 %collective-permute-start.5 = (f32[4,64,512]{2,1,0:T(8,128)}, f32[4,64,512]{2,1,0:T(8,128)}, u32[]{:S(2)}, u32[]{:S(2)}) collective-permute-start(f32[4,64,512]{2,1,0:T(8,128)} %gather_fusion.3), channel_id=1, source_target_pairs={{0,7},{1,0},{2,1},{3,2},{4,3},{5,4},{6,5},{7,6},{8,15},{9,8},{10,9... | collective-permute-start | bytes 1572872 | tf_op jit(solution)/shard_map/ppermute | solution.py:18
  20.0 16.5 %copy-start.8 = (s32[5,32]{1,0:T(8,128)S(1)}, s32[5,32]{1,0:T(8,128)}, u32[]{:S(2)}) copy-start(s32[5,32]{1,0:T(8,128)} %param.12) | copy-start | bytes 1924
  20.0 16.5 %copy-start.7 = (s32[5,32,4]{1,2,0:T(4,128)S(1)}, s32[5,32,4]{1,2,0:T(4,128)}, u32[]{:S(2)}) copy-start(s32[5,32,4]{1,2,0:T(4,128)} %param.11) | copy-start | bytes 7684
  20.1 17.6 %copy-start.6 = (f32[5,16,32]{2,1,0:T(8,128)S(1)}, f32[5,16,32]{2,1,0:T(8,128)}, u32[]{:S(2)}) copy-start(f32[5,16,32]{2,1,0:T(8,128)} %param.8) | copy-start | bytes 30724
  20.1 17.6 %copy-start = (f32[16,32,512]{2,1,0:T(8,128)S(1)}, f32[16,32,512]{2,1,0:T(8,128)}, u32[]{:S(2)}) copy-start(f32[16,32,512]{2,1,0:T(8,128)} %param.7) | copy-start | bytes 3145732
  23.7 71.8 %collective-permute-start.3 = (f32[4,64,512]{2,1,0:T(8,128)}, f32[4,64,512]{2,1,0:T(8,128)}, u32[]{:S(2)}, u32[]{:S(2)}) collective-permute-start(f32[4,64,512]{2,1,0:T(8,128)} %gather_fusion.1), channel_id=1, source_target_pairs={{0,24},{8,0},{16,8},{24,16},{1,25},{9,1},{17,9},{25,17},{2,26},{10... | collective-permute-start | bytes 1572872 | tf_op jit(solution)/shard_map/ppermute | solution.py:18
  31.7 62.0 %collective-permute-start.2 = (f32[4,64,512]{2,1,0:T(8,128)}, f32[4,64,512]{2,1,0:T(8,128)}, u32[]{:S(2)}, u32[]{:S(2)}) collective-permute-start(f32[4,64,512]{2,1,0:T(8,128)} %gather_fusion), channel_id=1, source_target_pairs={{0,8},{8,16},{16,24},{24,0},{1,9},{9,17},{17,25},{25,1},{2,10},{10... | collective-permute-start | bytes 1572872 | tf_op jit(solution)/shard_map/ppermute | solution.py:18
  78.8 18.6 %collective-permute-start.4 = (f32[4,64,512]{2,1,0:T(8,128)}, f32[4,64,512]{2,1,0:T(8,128)S(1)}, u32[]{:S(2)}, u32[]{:S(2)}) collective-permute-start(f32[4,64,512]{2,1,0:T(8,128)} %gather_fusion.2), channel_id=1, source_target_pairs={{0,1},{1,2},{2,3},{3,4},{4,5},{5,6},{6,7},{7,0},{8,9},{9,10},{10,1... | collective-permute-start | bytes 1572872 | tf_op jit(solution)/shard_map/ppermute | solution.py:18
  163.8 14.5 %copy-start.5 = (f32[32,64,512]{2,1,0:T(8,128)S(1)}, f32[32,64,512]{2,1,0:T(8,128)}, u32[]{:S(2)}) copy-start(f32[32,64,512]{2,1,0:T(8,128)} %param.9) | copy-start | bytes 12582916
  178.4 8.0 copy-start.4
  186.4 26.1 %slice-start.4 = ((s8[16777216]{0:T(1024)(128)(4,1)}), s8[4194304]{0:T(1024)(128)(4,1)S(1)}, s32[]{:S(2)}) async-start(s8[16777216]{0:T(1024)(128)(4,1)} %bitcast.209), calls=%async_computation.5 | async-start | bytes 8388608
  186.4 26.1 %slice-start.5 = ((s8[16777216]{0:T(1024)(128)(4,1)}), s8[4194304]{0:T(1024)(128)(4,1)S(1)}, s32[]{:S(2)}) async-start(s8[16777216]{0:T(1024)(128)(4,1)} %bitcast.209), calls=%async_computation.6 | async-start | bytes 8388608
  186.4 26.1 %slice-start.6 = ((s8[16777216]{0:T(1024)(128)(4,1)}), s8[4194304]{0:T(1024)(128)(4,1)S(1)}, s32[]{:S(2)}) async-start(s8[16777216]{0:T(1024)(128)(4,1)} %bitcast.209), calls=%async_computation.7 | async-start | bytes 8388608
  201.7 10.9 slice-start.7
  201.7 10.9 copy-start.3
  225.8 10.5 copy-start.2
  236.4 25.7 %slice-start = ((s8[16777216]{0:T(1024)(128)(4,1)}), s8[4194304]{0:T(1024)(128)(4,1)S(1)}, s32[]{:S(2)}) async-start(s8[16777216]{0:T(1024)(128)(4,1)} %bitcast.205), calls=%async_computation.1 | async-start | bytes 8388608
  236.4 25.7 %slice-start.1 = ((s8[16777216]{0:T(1024)(128)(4,1)}), s8[4194304]{0:T(1024)(128)(4,1)S(1)}, s32[]{:S(2)}) async-start(s8[16777216]{0:T(1024)(128)(4,1)} %bitcast.205), calls=%async_computation.2 | async-start | bytes 8388608
  236.4 25.7 %slice-start.2 = ((s8[16777216]{0:T(1024)(128)(4,1)}), s8[4194304]{0:T(1024)(128)(4,1)S(1)}, s32[]{:S(2)}) async-start(s8[16777216]{0:T(1024)(128)(4,1)} %bitcast.205), calls=%async_computation.3 | async-start | bytes 8388608
  251.7 10.4 slice-start.3
  251.7 10.4 copy-start.1
Sparse Core Ops, SparseCore 0:
  299.0 840.0 all-gather.1
